TPU v7x, 32 devices: a whole 2x2x4 slice. The times are simulated.
32 devices in a mesh: dp: 4 (over z), section: 2 (over x), mp: 4 (over y, core).
Axes of the slice: x: 2, y: 2, z: 4, core: 2. Of those that a mesh axis runs over, the one named last changes fastest.
Arguments:
- source_rows: bfloat16 [1024, 1024], P('dp', 'mp'), may hold values from -6 to 6
- value_weight: bfloat16 [2, 1024, 1024], P('section', None, 'mp'), may hold values from -0.1875 to 0.1875
- gate_weight: bfloat16 [2, 1024, 1024], P('section', None, 'mp'), may hold values from -0.1875 to 0.1875
- kernel_weight: bfloat16 [2, 1024, 496], P('section', None, 'mp'), may hold values from -0.1875 to 0.1875
- segment_ids: int32 [8, 128], P('dp'), may hold values from 0 to 3, never falling along the last dimension, each value on 1 to 64 neighbouring positions
- out_grad: bfloat16 [1024, 1024], P('dp', 'mp'), may hold values from -6 to 6
Outputs:
- value_grad: float32 [2, 1024, 1024], P('section', 'dp', 'mp')
- gate_grad: float32 [2, 1024, 1024], P('section', 'dp', 'mp')
- kernel_grad: float32 [2, 1024, 496], P('section', 'dp', 'mp')
Inputs may be any that keep to these rules, and one draw needn't show every extreme that they name: `segment_ids`: in each microbatch row of 128 positions the sentence numbers never fall and every number from 0 up to the largest appears; a sentence covers 1 to 64 positions, and in every microbatch exactly one sentence covers 64 positions.
All inputs are finite; a program needn't handle non-finite values.
Results may differ from a plain program's by a relative error of at most 0.015.
Values may be sent and summed in bfloat16 or wider, within the bound.
A program may use at most 64 MiB of HBM per device.

v0:
```python
import jax
import jax.numpy as jnp
from jax import lax
from jax.sharding import PartitionSpec as P

KERNEL = 31


def from_behind(value, axis, steps):
    count = lax.axis_size(axis)
    initial, last = (max(0, -steps), min(count, count - steps))
    return lax.ppermute(value, axis, [(source, source + steps) for source in range(initial, last)])


def make_table(segments):
    row_count = segments.shape[0]
    positions = jnp.arange(row_count, dtype=jnp.int32)
    offsets = positions[None, :] - positions[:, None] + KERNEL // 2
    same_doc = segments[:, None] == segments[None, :]
    tap_index = jnp.arange(KERNEL, dtype=jnp.int32)[:, None, None]
    return ((offsets[None] == tap_index) & same_doc[None]).astype(jnp.float32)


def normalize(rows_in):
    widened = rows_in.astype(jnp.float32)
    row_mean = jnp.mean(widened, axis=-1, keepdims=True)
    centred = widened - row_mean
    inv_std = lax.rsqrt(jnp.mean(centred * centred, axis=-1, keepdims=True) + 1e-05)
    normed = centred * inv_std
    return (normed, inv_std, normed.astype(jnp.bfloat16))


def forward_pieces(normed_b, band_table, weights):
    w_value, w_gate, w_kernel = weights
    row_count = normed_b.shape[0]
    value_proj = jnp.dot(normed_b, w_value, preferred_element_type=jnp.float32)
    gate_proj = jnp.dot(normed_b, w_gate, preferred_element_type=jnp.float32)
    gate_sig = jax.nn.sigmoid(gate_proj)
    gated = (value_proj * gate_sig).astype(jnp.bfloat16)
    head_count = w_kernel.shape[1] // KERNEL
    head_size = w_value.shape[1] // head_count
    logits = jnp.dot(normed_b, w_kernel, preferred_element_type=jnp.float32).reshape(
        row_count, head_count, KERNEL
    )
    exp_logits = jnp.exp(logits)
    taps = exp_logits / jnp.sum(exp_logits, axis=-1, keepdims=True)
    band_mat = jnp.einsum(
        "thj,jts->hts",
        taps.astype(jnp.bfloat16),
        band_table.astype(jnp.bfloat16),
        preferred_element_type=jnp.float32,
    ).astype(jnp.bfloat16)
    gated3 = gated.reshape(row_count, head_count, head_size)
    mixed = jnp.einsum(
        "hts,shd->thd", band_mat, gated3, preferred_element_type=jnp.float32
    ).reshape(row_count, -1)
    return (value_proj, gate_sig, gated3, taps, band_mat, mixed)


def layer_forward(full_rows, segments, weights, mp_index):
    normed, inv_std, normed_b = normalize(full_rows)
    pieces = forward_pieces(normed_b, make_table(segments), weights)
    half_width = weights[0].shape[1]
    own_part = lax.dynamic_slice_in_dim(
        full_rows.astype(jnp.float32), mp_index * half_width, half_width, 1
    )
    return (own_part + pieces[5]).astype(jnp.bfloat16)


def layer_backward(normed_b, segments, grad_out, weights):
    w_value, w_gate, w_kernel = weights
    band_table = make_table(segments)
    value_proj, gate_sig, gated3, taps, band_mat, mixed = forward_pieces(
        normed_b, band_table, weights
    )
    row_count, head_count, head_size = gated3.shape
    grad_mixed = grad_out.astype(jnp.bfloat16).reshape(row_count, head_count, head_size)
    grad_gated = jnp.einsum(
        "hts,thd->shd", band_mat, grad_mixed, preferred_element_type=jnp.float32
    ).reshape(row_count, -1)
    tap_outer = jnp.einsum("thd,shd->hts", grad_mixed, gated3, preferred_element_type=jnp.float32)
    grad_taps = jnp.einsum("hts,jts->thj", tap_outer, band_table)
    grad_logits = (
        (taps * (grad_taps - jnp.sum(taps * grad_taps, axis=-1, keepdims=True)))
        .astype(jnp.bfloat16)
        .reshape(row_count, -1)
    )
    grad_value = (grad_gated * gate_sig).astype(jnp.bfloat16)
    grad_gate = (grad_gated * value_proj * gate_sig * (1.0 - gate_sig)).astype(jnp.bfloat16)
    dims = (((1,), (1,)), ((), ()))
    grad_part = lax.dot_general(grad_value, w_value, dims, preferred_element_type=jnp.float32)
    grad_part = grad_part + lax.dot_general(
        grad_gate, w_gate, dims, preferred_element_type=jnp.float32
    )
    grad_part = grad_part + lax.dot_general(
        grad_logits, w_kernel, dims, preferred_element_type=jnp.float32
    )
    return (grad_part, jnp.concatenate([grad_value, grad_gate, grad_logits], axis=1))


def shards(source_rows, value_weight, gate_weight, kernel_weight, segment_ids, out_grad):
    section_count = lax.axis_size("section")
    section_index = lax.axis_index("section")
    mp_index = lax.axis_index("mp")
    micro_count, row_count = segment_ids.shape
    full_width = value_weight.shape[1]
    half_width = value_weight.shape[2]
    weights = (value_weight[0], gate_weight[0], kernel_weight[0])
    term_width = 2 * half_width + kernel_weight.shape[2]
    inputs = source_rows.reshape(micro_count, row_count, half_width)
    top_grads = out_grad.reshape(micro_count, row_count, half_width)
    tick_count = micro_count + section_count - 1

    def forward_tick(tick, carry):
        received, stored = carry
        micro_index = tick - section_index
        active = (micro_index >= 0) & (micro_index < micro_count)
        slot_index = jnp.clip(micro_index, 0, micro_count - 1)
        own_rows = jnp.where(section_index == 0, inputs[slot_index], received)
        full_rows = lax.all_gather(own_rows, "mp", axis=1, tiled=True)
        segments = segment_ids[slot_index]
        result = lax.cond(
            active,
            lambda: layer_forward(full_rows, segments, weights, mp_index),
            lambda: jnp.zeros_like(own_rows),
        )
        stored = stored.at[slot_index].set(jnp.where(active, full_rows, stored[slot_index]))
        passed = from_behind(result, "section", 1)
        return (passed, stored)

    start_rows = jnp.zeros((row_count, half_width), jnp.bfloat16)
    start_store = jnp.zeros((micro_count, row_count, full_width), jnp.bfloat16)
    unused, stored = lax.fori_loop(0, tick_count, forward_tick, (start_rows, start_store))

    def backward_tick(tick, carry):
        received, grads, terms_store = carry
        micro_index = tick - (section_count - 1 - section_index)
        active = (micro_index >= 0) & (micro_index < micro_count)
        slot_index = jnp.clip(micro_index, 0, micro_count - 1)
        top_grad = top_grads[slot_index].astype(jnp.float32)
        grad_out = jnp.where(section_index == section_count - 1, top_grad, received)
        segments = segment_ids[slot_index]
        normed, inv_std, normed_b = normalize(stored[slot_index])
        grad_part, grad_terms = lax.cond(
            active,
            lambda: layer_backward(normed_b, segments, grad_out, weights),
            lambda: (
                jnp.zeros((row_count, full_width), jnp.float32),
                jnp.zeros((row_count, term_width), jnp.bfloat16),
            ),
        )
        grad_normed = lax.psum(grad_part.astype(jnp.bfloat16), "mp").astype(jnp.float32)
        norm_back = inv_std * (
            grad_normed
            - jnp.mean(grad_normed, axis=-1, keepdims=True)
            - normed * jnp.mean(grad_normed * normed, axis=-1, keepdims=True)
        )
        own_back = lax.dynamic_slice_in_dim(norm_back, mp_index * half_width, half_width, 1)
        grad_in = grad_out + own_back
        grad_in = jnp.where(active, grad_in, 0.0)
        grads = lax.cond(
            active,
            lambda: grads
            + lax.dot_general(
                normed_b, grad_terms, (((0,), (0,)), ((), ())), preferred_element_type=jnp.float32
            ),
            lambda: grads,
        )
        passed = from_behind(grad_in.astype(jnp.bfloat16), "section", -1).astype(grad_in.dtype)
        return (passed, grads, terms_store)

    start_grads = jnp.zeros((full_width, term_width), jnp.float32)
    start_terms = jnp.zeros((1,), jnp.bfloat16)
    start_back = jnp.zeros((row_count, half_width), jnp.float32)
    unused, grads, terms_store = lax.fori_loop(
        0, tick_count, backward_tick, (start_back, start_grads, start_terms)
    )
    shares = lax.psum_scatter(
        grads.astype(jnp.bfloat16), "dp", scatter_dimension=0, tiled=True
    ).astype(jnp.float32)
    value_share = shares[:, :half_width][None]
    gate_share = shares[:, half_width : 2 * half_width][None]
    kernel_share = shares[:, 2 * half_width :][None]
    return (value_share, gate_share, kernel_share)


def solution(mesh):
    in_specs = (
        P("dp", "mp"),
        P("section", None, "mp"),
        P("section", None, "mp"),
        P("section", None, "mp"),
        P("dp", None),
        P("dp", "mp"),
    )
    out_specs = (P("section", "dp", "mp"), P("section", "dp", "mp"), P("section", "dp", "mp"))
    return jax.shard_map(shards, mesh=mesh, in_specs=in_specs, out_specs=out_specs, check_vma=False)
```

profile of v0, /device:TPU:0, one launch (start us, length us, event | category | flops | bytes accessed | tf_op | source)
XLA Modules:
  0.0 359.8 jit_solution(7524102810339772016)
XLA Ops:
  8.1 50.1 %while.38 = (s32[]{:T(128)}, bf16[128,256]{0,1:T(8,128)(2,1)S(1)}, bf16[2,128,1024]{1,2,0:T(8,128)(2,1)S(1)}, s32[]{:T(128)}, pred[]{:T(512)}, /*index=5*/bf16[2...) while((s32[]{:T(128)}, bf16[128,256]{0,1:T(8,128)(2,1)S(1)}, ...), condition=%wide.region_7.8_spmd, body=%wide.region_0.7_spmd.sunk | while | flops 184383632 | bytes 11819549 | solution.py:133
  9.1 7.2 %all_gather.9 = bf16[128,1024]{0,1:T(8,128)(2,1)S(1)} all-gather(bf16[128,256]{0,1:T(8,128)(2,1)S(1)} %bitcast_select_fusion.4), channel_id=1, replica_groups=mesh['dp'=4,'section'=2,'mp'=4] {'mp'}, dimensions={1}, use_global_device_ids=true | all-gather | bytes 327680 | tf_op jit(solution)/shard_map/while/body/eval_jaxpr/all_gather | solution.py:120
  16.4 4.1 %conditional.8 = (bf16[128,256]{0,1:T(8,128)(2,1)S(1)}) conditional(s32[]{:T(128)} %convert_element_type.241, () %tuple.133, (bf16[128,1024]{0,1:T(8,128)(2,1)S(1)}, s32[]{:T(128)}, bf16[1024,256]{1,0:T(8,128)(2,1)}, bf16[1024,256]{1,0:T(8,128)(2,1)}, s32[2,128]{1,0:T(2,128)}, /*index=5*/s32[]{:T(128)}, bf16[1024,124]{1,0:T(8,128)(2,1)}) %tuple.134), branch_computations={%region_1.1_spmd, %region_2.5_spmd} | conditional | flops 184088704 | bytes 9459834 | solution.py:122
  24.9 5.8 %all_gather.9 = bf16[128,1024]{0,1:T(8,128)(2,1)S(1)} all-gather(bf16[128,256]{0,1:T(8,128)(2,1)S(1)} %bitcast_select_fusion.4), channel_id=1, replica_groups=mesh['dp'=4,'section'=2,'mp'=4] {'mp'}, dimensions={1}, use_global_device_ids=true | all-gather | bytes 327680 | tf_op jit(solution)/shard_map/while/body/eval_jaxpr/all_gather | solution.py:120
  30.7 4.1 %conditional.8 = (bf16[128,256]{0,1:T(8,128)(2,1)S(1)}) conditional(s32[]{:T(128)} %convert_element_type.241, () %tuple.133, (bf16[128,1024]{0,1:T(8,128)(2,1)S(1)}, s32[]{:T(128)}, bf16[1024,256]{1,0:T(8,128)(2,1)}, bf16[1024,256]{1,0:T(8,128)(2,1)}, s32[2,128]{1,0:T(2,128)}, /*index=5*/s32[]{:T(128)}, bf16[1024,124]{1,0:T(8,128)(2,1)}) %tuple.134), branch_computations={%region_1.1_spmd, %region_2.5_spmd} | conditional | flops 184088704 | bytes 9459834 | solution.py:122
  34.8 4.4 %collective-permute-start = (bf16[128,256]{0,1:T(8,128)(2,1)S(1)}, bf16[128,256]{0,1:T(8,128)(2,1)S(1)}, u32[]{:S(2)}, u32[]{:S(2)}) collective-permute-start(bf16[128,256]{0,1:T(8,128)(2,1)S(1)} %get-tuple-element.1041), channel_id=1, source_target_pairs={{0,4},{1,5},{2,6},{3,7},{8,12},{9,13},{10,14},{11,15},{16,20},{17,... | collective-permute-start | bytes 196616 | tf_op jit(solution)/shard_map/while/body/eval_jaxpr/ppermute | solution.py:12
  42.1 5.8 %all_gather.9 = bf16[128,1024]{0,1:T(8,128)(2,1)S(1)} all-gather(bf16[128,256]{0,1:T(8,128)(2,1)S(1)} %bitcast_select_fusion.4), channel_id=1, replica_groups=mesh['dp'=4,'section'=2,'mp'=4] {'mp'}, dimensions={1}, use_global_device_ids=true | all-gather | bytes 327680 | tf_op jit(solution)/shard_map/while/body/eval_jaxpr/all_gather | solution.py:120
  47.9 8.5 %collective-permute-start = (bf16[128,256]{0,1:T(8,128)(2,1)S(1)}, bf16[128,256]{0,1:T(8,128)(2,1)S(1)}, u32[]{:S(2)}, u32[]{:S(2)}) collective-permute-start(bf16[128,256]{0,1:T(8,128)(2,1)S(1)} %get-tuple-element.1041), channel_id=1, source_target_pairs={{0,4},{1,5},{2,6},{3,7},{8,12},{9,13},{10,14},{11,15},{16,20},{17,... | collective-permute-start | bytes 196616 | tf_op jit(solution)/shard_map/while/body/eval_jaxpr/ppermute | solution.py:12
  59.5 257.4 %while.39 = (s32[]{:T(128)}, f32[128,256]{1,0:T(8,128)}, f32[1024,636]{1,0:T(8,128)S(1)}, s32[]{:T(128)}, pred[]{:T(512)}, /*index=5*/bf16[2,128,256]{2,1,0:T(8,...) while((s32[]{:T(128)}, f32[128,256]{1,0:T(8,128)}, ...), condition=%wide.region_20.21_spmd.clone, body=%wide.region_8.20_spmd.clone.sunk | while | flops 533156512 | bytes 23325744 | solution.py:175
  65.9 71.7 %all-reduce.2.cloned.1.call-done = bf16[128,1024]{1,0:T(8,128)(2,1)} async-done(((bf16[128,1024]{1,0:T(8,128)(2,1)}), bf16[128,1024]{1,0:T(8,128)(2,1)}) %all-reduce.2.cloned.1.call-update) | async-done | bytes 262160 | tf_op jit(solution)/shard_map/while/body/eval_jaxpr/psum | solution.py:152
  141.8 4.8 %collective-permute-done.1 = bf16[128,256]{1,0:T(8,128)(2,1)S(1)} collective-permute-done((bf16[128,256]{1,0:T(8,128)(2,1)S(1)}, bf16[128,256]{1,0:T(8,128)(2,1)S(1)}, u32[]{:S(2)}, u32[]{:S(2)}) %collective-permute-start.1) | collective-permute-done | bytes 65568 | tf_op jit(solution)/shard_map/while/body/eval_jaxpr/ppermute | solution.py:12
  152.3 38.8 %conditional.9 = (bf16[128,1024]{1,0:T(8,128)(2,1)}, bf16[128,636]{1,0:T(8,128)(2,1)}) conditional(s32[]{:T(128)} %convert_element_type.248, () %tuple.138, (s32[2,128]{1,0:T(2,128)}, s32[]{:T(128)}, bf16[128,1024]{1,0:T(8,128)(2,1)}, bf16[1024,124]{1,0:T(8,128)(2,1)}, f32[128,256]{1,0:T(8,128)S(1)}, /*index=5*/bf16[1024,256]{1,0:T(8,128)(2,1)}, ...), branch_computations={%region_11.11_spmd, %region_12.14_spmd} | conditional | flops 362930720 | bytes 10925676 | solution.py:144
  154.5 1.9 convolution_exponential_fusion.1
  160.7 2.0 fusion.23
  168.4 2.0 multiply_convert_fusion.4
  172.0 1.8 convolution_bitcast_fusion
  176.9 7.4 %fusion.20 = bf16[128,4,31]{2,1,0:T(4,128)(2,1)} fusion(f32[128,4,31]{2,1,0:T(4,128)S(1)} %fusion.16, f32[128,4,31]{2,1,0:T(4,128)} %copy.31, f32[128,4]{1,0:T(8,128)} %copy.30), kind=kOutput, calls=%fused_computation.45 | output fusion | flops 95774 | bytes 160768 | tf_op jit(solution)/shard_map/while/body/eval_jaxpr/cond/branch_1_fun/sub | solution.py:84
  191.1 31.2 %all-reduce.2.cloned.1.call-done = bf16[128,1024]{1,0:T(8,128)(2,1)} async-done(((bf16[128,1024]{1,0:T(8,128)(2,1)}), bf16[128,1024]{1,0:T(8,128)(2,1)}) %all-reduce.2.cloned.1.call-update) | async-done | bytes 262160 | tf_op jit(solution)/shard_map/while/body/eval_jaxpr/psum | solution.py:152
  226.6 1.7 conditional.10
  226.6 1.7 convolution_add_fusion.2
  228.3 3.1 collective-permute-done.1
  237.1 38.8 %conditional.9 = (bf16[128,1024]{1,0:T(8,128)(2,1)}, bf16[128,636]{1,0:T(8,128)(2,1)}) conditional(s32[]{:T(128)} %convert_element_type.248, () %tuple.138, (s32[2,128]{1,0:T(2,128)}, s32[]{:T(128)}, bf16[128,1024]{1,0:T(8,128)(2,1)}, bf16[1024,124]{1,0:T(8,128)(2,1)}, f32[128,256]{1,0:T(8,128)S(1)}, /*index=5*/bf16[1024,256]{1,0:T(8,128)(2,1)}, ...), branch_computations={%region_11.11_spmd, %region_12.14_spmd} | conditional | flops 362930720 | bytes 10925676 | solution.py:144
  239.3 1.9 convolution_exponential_fusion.1
  245.5 2.0 fusion.23
  253.2 2.0 multiply_convert_fusion.4
  256.8 1.8 convolution_bitcast_fusion
  261.7 7.4 %fusion.20 = bf16[128,4,31]{2,1,0:T(4,128)(2,1)} fusion(f32[128,4,31]{2,1,0:T(4,128)S(1)} %fusion.16, f32[128,4,31]{2,1,0:T(4,128)} %copy.31, f32[128,4]{1,0:T(8,128)} %copy.30), kind=kOutput, calls=%fused_computation.45 | output fusion | flops 95774 | bytes 160768 | tf_op jit(solution)/shard_map/while/body/eval_jaxpr/cond/branch_1_fun/sub | solution.py:84
  275.9 31.2 %all-reduce.2.cloned.1.call-done = bf16[128,1024]{1,0:T(8,128)(2,1)} async-done(((bf16[128,1024]{1,0:T(8,128)(2,1)}), bf16[128,1024]{1,0:T(8,128)(2,1)}) %all-reduce.2.cloned.1.call-update) | async-done | bytes 262160 | tf_op jit(solution)/shard_map/while/body/eval_jaxpr/psum | solution.py:152
  311.4 1.7 conditional.10
  311.4 1.7 convolution_add_fusion.2
  313.1 3.1 collective-permute-done.1
  318.2 31.9 %reduce-scatter.2.cloned.1.call-done = bf16[256,636]{1,0:T(8,128)(2,1)} async-done(((bf16[1024,636]{1,0:T(8,128)(2,1)}), bf16[256,636]{1,0:T(8,128)(2,1)}) %reduce-scatter.2.cloned.1.call-update) | async-done | bytes 325648 | tf_op jit(solution)/shard_map/reduce_scatter | solution.py:178
  (205 shorter events, 102.9 us)
Async XLA Ops:
  16.4 5.5 %copy-start.9 = (s32[3]{0:T(128)S(1)}, s32[3]{0:T(128)}, u32[]{:S(2)}) copy-start(s32[3]{0:T(128)} %get-tuple-element.994) | copy-start | bytes 40 | tf_op jit(solution)/shard_map/while
  16.4 3.2 copy-start
  16.4 3.4 copy-start.5
  20.5 3.4 collective-permute-start
  30.7 8.6 %copy-start.9 = (s32[3]{0:T(128)S(1)}, s32[3]{0:T(128)}, u32[]{:S(2)}) copy-start(s32[3]{0:T(128)} %get-tuple-element.994) | copy-start | bytes 40 | tf_op jit(solution)/shard_map/while
  30.7 3.2 copy-start
  30.7 3.4 copy-start.5
  34.8 6.3 %collective-permute-start = (bf16[128,256]{0,1:T(8,128)(2,1)S(1)}, bf16[128,256]{0,1:T(8,128)(2,1)S(1)}, u32[]{:S(2)}, u32[]{:S(2)}) collective-permute-start(bf16[128,256]{0,1:T(8,128)(2,1)S(1)} %get-tuple-element.1041), channel_id=1, source_target_pairs={{0,4},{1,5},{2,6},{3,7},{8,12},{9,13},{10,14},{11,15},{16,20},{17,... | collective-permute-start | bytes 196616 | tf_op jit(solution)/shard_map/while/body/eval_jaxpr/ppermute | solution.py:12
  47.9 8.5 %copy-start.9 = (s32[3]{0:T(128)S(1)}, s32[3]{0:T(128)}, u32[]{:S(2)}) copy-start(s32[3]{0:T(128)} %get-tuple-element.994) | copy-start | bytes 40 | tf_op jit(solution)/shard_map/while
  47.9 10.4 %collective-permute-start = (bf16[128,256]{0,1:T(8,128)(2,1)S(1)}, bf16[128,256]{0,1:T(8,128)(2,1)S(1)}, u32[]{:S(2)}, u32[]{:S(2)}) collective-permute-start(bf16[128,256]{0,1:T(8,128)(2,1)S(1)} %get-tuple-element.1041), channel_id=1, source_target_pairs={{0,4},{1,5},{2,6},{3,7},{8,12},{9,13},{10,14},{11,15},{16,20},{17,... | collective-permute-start | bytes 196616 | tf_op jit(solution)/shard_map/while/body/eval_jaxpr/ppermute | solution.py:12
  58.3 0.8 copy-start.3
  58.3 1.2 copy-start.1
  59.5 78.1 %all-reduce.2.cloned.1.call-start = ((), (), s32[]{:S(2)}) async-start(), calls=%async_computation.2 | async-start | bytes 524288 | tf_op jit(solution)/shard_map/while/body/eval_jaxpr/psum | solution.py:152
  62.4 1.2 copy-start.7
  62.6 0.9 copy-start.8
  140.5 6.2 %collective-permute-start.1 = (bf16[128,256]{1,0:T(8,128)(2,1)S(1)}, bf16[128,256]{1,0:T(8,128)(2,1)S(1)}, u32[]{:S(2)}, u32[]{:S(2)}) collective-permute-start(bf16[128,256]{1,0:T(8,128)(2,1)S(1)} %fusion.74), channel_id=1, source_target_pairs={{4,0},{5,1},{6,2},{7,3},{12,8},{13,9},{14,10},{15,11},{20,16},{21,... | collective-permute-start | bytes 196616 | tf_op jit(solution)/shard_map/while/body/eval_jaxpr/ppermute | solution.py:12
  147.3 75.0 %all-reduce.2.cloned.1.call-start = ((), (), s32[]{:S(2)}) async-start(), calls=%async_computation.2 | async-start | bytes 524288 | tf_op jit(solution)/shard_map/while/body/eval_jaxpr/psum | solution.py:152
  150.2 1.2 copy-start.7
  150.5 0.9 copy-start.8
  164.4 1.5 copy-start.4
  186.0 4.2 %copy-start.2 = (bf16[1024,124]{1,0:T(8,128)(2,1)S(1)}, bf16[1024,124]{1,0:T(8,128)(2,1)}, u32[]{:S(2)}) copy-start(bf16[1024,124]{1,0:T(8,128)(2,1)} %get-tuple-element.579) | copy-start | bytes 761860 | tf_op jit(solution)/shard_map/while/body/eval_jaxpr/cond
  186.0 4.2 %copy-start.6 = (bf16[128,124]{1,0:T(8,128)(2,1)S(1)}, bf16[128,124]{1,0:T(8,128)(2,1)}, u32[]{:S(2)}) copy-start(bf16[128,124]{1,0:T(8,128)(2,1)} %reshape.248) | copy-start | bytes 95236 | tf_op jit(solution)/shard_map/while/body/eval_jaxpr/cond
  225.3 6.2 %collective-permute-start.1 = (bf16[128,256]{1,0:T(8,128)(2,1)S(1)}, bf16[128,256]{1,0:T(8,128)(2,1)S(1)}, u32[]{:S(2)}, u32[]{:S(2)}) collective-permute-start(bf16[128,256]{1,0:T(8,128)(2,1)S(1)} %fusion.74), channel_id=1, source_target_pairs={{4,0},{5,1},{6,2},{7,3},{12,8},{13,9},{14,10},{15,11},{20,16},{21,... | collective-permute-start | bytes 196616 | tf_op jit(solution)/shard_map/while/body/eval_jaxpr/ppermute | solution.py:12
  232.1 75.0 %all-reduce.2.cloned.1.call-start = ((), (), s32[]{:S(2)}) async-start(), calls=%async_computation.2 | async-start | bytes 524288 | tf_op jit(solution)/shard_map/while/body/eval_jaxpr/psum | solution.py:152
  235.0 1.2 copy-start.7
  235.3 0.9 copy-start.8
  249.2 1.5 copy-start.4
  270.8 4.2 %copy-start.2 = (bf16[1024,124]{1,0:T(8,128)(2,1)S(1)}, bf16[1024,124]{1,0:T(8,128)(2,1)}, u32[]{:S(2)}) copy-start(bf16[1024,124]{1,0:T(8,128)(2,1)} %get-tuple-element.579) | copy-start | bytes 761860 | tf_op jit(solution)/shard_map/while/body/eval_jaxpr/cond
  270.8 4.2 %copy-start.6 = (bf16[128,124]{1,0:T(8,128)(2,1)S(1)}, bf16[128,124]{1,0:T(8,128)(2,1)}, u32[]{:S(2)}) copy-start(bf16[128,124]{1,0:T(8,128)(2,1)} %reshape.248) | copy-start | bytes 95236 | tf_op jit(solution)/shard_map/while/body/eval_jaxpr/cond
  310.1 6.2 %collective-permute-start.1 = (bf16[128,256]{1,0:T(8,128)(2,1)S(1)}, bf16[128,256]{1,0:T(8,128)(2,1)S(1)}, u32[]{:S(2)}, u32[]{:S(2)}) collective-permute-start(bf16[128,256]{1,0:T(8,128)(2,1)S(1)} %fusion.74), channel_id=1, source_target_pairs={{4,0},{5,1},{6,2},{7,3},{12,8},{13,9},{14,10},{15,11},{20,16},{21,... | collective-permute-start | bytes 196616 | tf_op jit(solution)/shard_map/while/body/eval_jaxpr/ppermute | solution.py:12
  316.9 33.1 %reduce-scatter.2.cloned.1.call-start = ((), (), s32[]{:S(2)}) async-start(), calls=%async_computation.1 | async-start | bytes 1638400 | tf_op jit(solution)/shard_map/reduce_scatter | solution.py:178
Sparse Core Ops, SparseCore 0:
  66.0 71.5 all-reduce.1
  191.3 31.0 all-reduce.1
  276.0 31.0 all-reduce.1
Sparse Core Ops, SparseCore 1:
  319.7 30.3 reduce-scatter.1
where the time goes:
time: 362 us; the launch traced here: 360 us
  waiting for transfers between devices  179 us (49%)
  other arithmetic  47.1 us (13%)
  local copies, waits for them, and re-layouts  42.7 us (12%)
  matrix products  38.4 us (11%)
  blocking collectives  18.8 us (5%)
  starting transfers between devices  18 us (5%)
  between operations  15.2 us (4%)
    psum x3, waiting for transfers between devices, backward_tick(): lax.psum(grad_part.astype(jnp.bfloat16), 'mp').astype(jnp.float32)  134 us
    reduce_scatter x1, waiting for transfers between devices, shards(): lax.psum_scatter(grads.astype(jnp.bfloat16), 'dp', scatter_dimension=0, t...  31.9 us
    all_gather x3, blocking collectives, forward_tick(): full_rows = lax.all_gather(own_rows, 'mp', axis=1, tiled=True)  18.8 us
    ppermute x6, starting transfers between devices, from_behind(): lax.ppermute(value, axis, [(source, source + steps) for source in range(i...  18 us
    sub x2, other arithmetic, layer_backward(): grad_taps - jnp.sum(taps * grad_taps, axis=-1, keepdims=True)  14.8 us
    ppermute x6, waiting for transfers between devices, from_behind(): lax.ppermute(value, axis, [(source, source + steps) for source in range(i...  12.7 us
    dynamic_slice x6, local copies, waits for them, and re-layouts, backward_tick(): normed, inv_std, normed_b = normalize(stored[slot_index])  8.26 us
  transfers between devices with their start and end apart: 10, of which 10 were waited for; matrix products, arithmetic and copies ran while one was open for 2% of the time, Pallas kernels for 0%

commit v1 on v0

--- a/solution.py
+++ b/solution.py
@@ -117,7 +117,14 @@
         active = (micro_index >= 0) & (micro_index < micro_count)
         slot_index = jnp.clip(micro_index, 0, micro_count - 1)
         own_rows = jnp.where(section_index == 0, inputs[slot_index], received)
-        full_rows = lax.all_gather(own_rows, "mp", axis=1, tiled=True)
+        n_dev = lax.axis_size("mp")
+        right = [(i, (i + 1) % n_dev) for i in range(n_dev)]
+        parts = [own_rows]
+        for hop in range(1, n_dev):
+            parts = [lax.ppermute(parts[0], "mp", right), *parts]
+        out = jnp.concatenate(parts, axis=1)
+        shift = (lax.axis_index("mp") + 1) * parts[-1].shape[1]
+        full_rows = jnp.roll(out, shift, axis=1)
         segments = segment_ids[slot_index]
         result = lax.cond(
             active,

time: 362 us -> 376 us (1.039)
  waiting for transfers between devices: 179 us -> 212 us
  blocking collectives: 18.8 us -> 0 us
    ppermute x0 -> x9, waiting for transfers between devices: none -> 28.8 us  [forward_tick(): parts = [lax.ppermute(parts[0], 'mp', right), *parts]]
    all_gather x3 -> x0, blocking collectives: 18.8 us -> none  [forward_tick(): full_rows = lax.all_gather(own_rows, 'mp', axis=1, tiled=True)]
    ppermute x6, waiting for transfers between devices: 12.7 us -> 16.7 us  [from_behind(): lax.ppermute(value, axis, [(source, source + steps) for source in range(i...]
  transfers between devices with their start and end apart: 10 -> 19, of which waited for: 10 -> 19; matrix products, arithmetic and copies ran while one was open for 2% -> 2% of each run, Pallas kernels for 0% -> 0%
where the time goes in v1:
time: 376 us; the launch traced here: 374 us
  waiting for transfers between devices  212 us (56%)
  other arithmetic  49.8 us (13%)
  local copies, waits for them, and re-layouts  41.8 us (11%)
  matrix products  36.5 us (10%)
  starting transfers between devices  17.4 us (5%)
  between operations  15.2 us (4%)
    psum x3, waiting for transfers between devices, backward_tick(): lax.psum(grad_part.astype(jnp.bfloat16), 'mp').astype(jnp.float32)  134 us
    reduce_scatter x1, waiting for transfers between devices, shards(): lax.psum_scatter(grads.astype(jnp.bfloat16), 'dp', scatter_dimension=0, t...  31.9 us
    ppermute x9, waiting for transfers between devices, forward_tick(): parts = [lax.ppermute(parts[0], 'mp', right), *parts]  28.8 us
    ppermute x6, waiting for transfers between devices, from_behind(): lax.ppermute(value, axis, [(source, source + steps) for source in range(i...  16.7 us
    ppermute x6, starting transfers between devices, from_behind(): lax.ppermute(value, axis, [(source, source + steps) for source in range(i...  16.6 us
    sub x2, other arithmetic, layer_backward(): grad_taps - jnp.sum(taps * grad_taps, axis=-1, keepdims=True)  14.8 us
    dynamic_slice x6, local copies, waits for them, and re-layouts, backward_tick(): normed, inv_std, normed_b = normalize(stored[slot_index])  8.26 us
  transfers between devices with their start and end apart: 19, of which 19 were waited for; matrix products, arithmetic and copies ran while one was open for 2% of the time, Pallas kernels for 0%

profile of v1, /device:TPU:0, one launch (start us, length us, event | category | flops | bytes accessed | tf_op | source)
XLA Modules:
  0.0 373.6 jit_solution(9869580517176159733)
XLA Ops:
  8.1 63.7 %while.39 = (s32[]{:T(128)}, bf16[128,256]{0,1:T(8,128)(2,1)S(1)}, bf16[2,128,1024]{1,2,0:T(8,128)(2,1)S(1)}, s32[]{:T(128)}, pred[]{:T(512)}, /*index=5*/bf16[2...) while((s32[]{:T(128)}, bf16[128,256]{0,1:T(8,128)(2,1)S(1)}, ...), condition=%wide.region_7.8_spmd, body=%wide.region_0.7_spmd.sunk | while | flops 184383664 | bytes 14609268 | solution.py:140
  9.8 3.9 %collective-permute-done = bf16[128,256]{0,1:T(8,128)(2,1)S(1)} collective-permute-done((bf16[128,256]{0,1:T(8,128)(2,1)S(1)}, bf16[128,256]{0,1:T(8,128)(2,1)S(1)}, u32[]{:S(2)}, u32[]{:S(2)}) %collective-permute-start) | collective-permute-done | bytes 65568 | tf_op jit(solution)/shard_map/while/body/eval_jaxpr/ppermute | solution.py:124
  13.8 3.6 collective-permute-done.1
  18.9 2.2 collective-permute-done.2
  22.1 2.4 conditional.8
  29.4 3.6 collective-permute-done
  33.0 3.7 collective-permute-done.1
  38.2 2.2 collective-permute-done.2
  41.4 2.4 conditional.8
  43.8 4.3 %collective-permute-start.3 = (bf16[128,256]{0,1:T(8,128)(2,1)S(1)}, bf16[128,256]{0,1:T(8,128)(2,1)S(1)}, u32[]{:S(2)}, u32[]{:S(2)}) collective-permute-start(bf16[128,256]{0,1:T(8,128)(2,1)S(1)} %get-tuple-element.1100), channel_id=1, source_target_pairs={{0,4},{1,5},{2,6},{3,7},{8,12},{9,13},{10,14},{11,15},{16,20},{17,... | collective-permute-start | bytes 196616 | tf_op jit(solution)/shard_map/while/body/eval_jaxpr/ppermute | solution.py:12
  51.2 3.6 collective-permute-done
  54.9 3.7 collective-permute-done.1
  60.0 2.2 collective-permute-done.2
  63.3 6.7 %collective-permute-start.3 = (bf16[128,256]{0,1:T(8,128)(2,1)S(1)}, bf16[128,256]{0,1:T(8,128)(2,1)S(1)}, u32[]{:S(2)}, u32[]{:S(2)}) collective-permute-start(bf16[128,256]{0,1:T(8,128)(2,1)S(1)} %get-tuple-element.1100), channel_id=1, source_target_pairs={{0,4},{1,5},{2,6},{3,7},{8,12},{9,13},{10,14},{11,15},{16,20},{17,... | collective-permute-start | bytes 196616 | tf_op jit(solution)/shard_map/while/body/eval_jaxpr/ppermute | solution.py:12
  73.1 257.6 %while.40 = (s32[]{:T(128)}, f32[128,256]{1,0:T(8,128)}, f32[1024,636]{1,0:T(8,128)S(1)}, s32[]{:T(128)}, pred[]{:T(512)}, /*index=5*/bf16[2,128,256]{2,1,0:T(8,...) while((s32[]{:T(128)}, f32[128,256]{1,0:T(8,128)}, ...), condition=%wide.region_20.21_spmd.clone, body=%wide.region_8.20_spmd.clone.sunk | while | flops 533156512 | bytes 23325744 | solution.py:182
  79.5 71.9 %all-reduce.2.cloned.1.call-done = bf16[128,1024]{1,0:T(8,128)(2,1)} async-done(((bf16[128,1024]{1,0:T(8,128)(2,1)}), bf16[128,1024]{1,0:T(8,128)(2,1)}) %all-reduce.2.cloned.1.call-update) | async-done | bytes 262160 | tf_op jit(solution)/shard_map/while/body/eval_jaxpr/psum | solution.py:159
  155.6 4.8 %collective-permute-done.4 = bf16[128,256]{1,0:T(8,128)(2,1)S(1)} collective-permute-done((bf16[128,256]{1,0:T(8,128)(2,1)S(1)}, bf16[128,256]{1,0:T(8,128)(2,1)S(1)}, u32[]{:S(2)}, u32[]{:S(2)}) %collective-permute-start.4) | collective-permute-done | bytes 65568 | tf_op jit(solution)/shard_map/while/body/eval_jaxpr/ppermute | solution.py:12
  166.1 38.8 %conditional.9 = (bf16[128,1024]{1,0:T(8,128)(2,1)}, bf16[128,636]{1,0:T(8,128)(2,1)}) conditional(s32[]{:T(128)} %convert_element_type.250, () %tuple.145, (s32[2,128]{1,0:T(2,128)}, s32[]{:T(128)}, bf16[128,1024]{1,0:T(8,128)(2,1)}, bf16[1024,124]{1,0:T(8,128)(2,1)}, f32[128,256]{1,0:T(8,128)S(1)}, /*index=5*/bf16[1024,256]{1,0:T(8,128)(2,1)}, ...), branch_computations={%region_11.11_spmd, %region_12.14_spmd} | conditional | flops 362930720 | bytes 10925676 | solution.py:151
  168.3 1.9 convolution_exponential_fusion.1
  174.5 2.0 fusion.23
  182.2 2.0 multiply_convert_fusion.4
  190.7 7.4 %fusion.20 = bf16[128,4,31]{2,1,0:T(4,128)(2,1)} fusion(f32[128,4,31]{2,1,0:T(4,128)S(1)} %fusion.16, f32[128,4,31]{2,1,0:T(4,128)} %copy.31, f32[128,4]{1,0:T(8,128)} %copy.30), kind=kOutput, calls=%fused_computation.54 | output fusion | flops 95774 | bytes 160768 | tf_op jit(solution)/shard_map/while/body/eval_jaxpr/cond/branch_1_fun/sub | solution.py:84
  204.9 31.2 %all-reduce.2.cloned.1.call-done = bf16[128,1024]{1,0:T(8,128)(2,1)} async-done(((bf16[128,1024]{1,0:T(8,128)(2,1)}), bf16[128,1024]{1,0:T(8,128)(2,1)}) %all-reduce.2.cloned.1.call-update) | async-done | bytes 262160 | tf_op jit(solution)/shard_map/while/body/eval_jaxpr/psum | solution.py:159
  242.2 3.1 collective-permute-done.4
  250.9 38.8 %conditional.9 = (bf16[128,1024]{1,0:T(8,128)(2,1)}, bf16[128,636]{1,0:T(8,128)(2,1)}) conditional(s32[]{:T(128)} %convert_element_type.250, () %tuple.145, (s32[2,128]{1,0:T(2,128)}, s32[]{:T(128)}, bf16[128,1024]{1,0:T(8,128)(2,1)}, bf16[1024,124]{1,0:T(8,128)(2,1)}, f32[128,256]{1,0:T(8,128)S(1)}, /*index=5*/bf16[1024,256]{1,0:T(8,128)(2,1)}, ...), branch_computations={%region_11.11_spmd, %region_12.14_spmd} | conditional | flops 362930720 | bytes 10925676 | solution.py:151
  253.1 1.9 convolution_exponential_fusion.1
  259.4 2.0 fusion.23
  267.1 2.0 multiply_convert_fusion.4
  275.6 7.4 %fusion.20 = bf16[128,4,31]{2,1,0:T(4,128)(2,1)} fusion(f32[128,4,31]{2,1,0:T(4,128)S(1)} %fusion.16, f32[128,4,31]{2,1,0:T(4,128)} %copy.31, f32[128,4]{1,0:T(8,128)} %copy.30), kind=kOutput, calls=%fused_computation.54 | output fusion | flops 95774 | bytes 160768 | tf_op jit(solution)/shard_map/while/body/eval_jaxpr/cond/branch_1_fun/sub | solution.py:84
  289.8 31.2 %all-reduce.2.cloned.1.call-done = bf16[128,1024]{1,0:T(8,128)(2,1)} async-done(((bf16[128,1024]{1,0:T(8,128)(2,1)}), bf16[128,1024]{1,0:T(8,128)(2,1)}) %all-reduce.2.cloned.1.call-update) | async-done | bytes 262160 | tf_op jit(solution)/shard_map/while/body/eval_jaxpr/psum | solution.py:159
  326.9 3.1 collective-permute-done.4
  332.0 31.9 %reduce-scatter.2.cloned.1.call-done = bf16[256,636]{1,0:T(8,128)(2,1)} async-done(((bf16[1024,636]{1,0:T(8,128)(2,1)}), bf16[256,636]{1,0:T(8,128)(2,1)}) %reduce-scatter.2.cloned.1.call-update) | async-done | bytes 325648 | tf_op jit(solution)/shard_map/reduce_scatter | solution.py:185
  (254 shorter events, 118.4 us)
Async XLA Ops:
  8.1 13.9 %copy-start = (bf16[1024,256]{1,0:T(8,128)(2,1)S(1)}, bf16[1024,256]{1,0:T(8,128)(2,1)}, u32[]{:S(2)}) copy-start(bf16[1024,256]{1,0:T(8,128)(2,1)} %get-tuple-element.1041) | copy-start | bytes 1572868 | tf_op jit(solution)/shard_map/while
  8.1 13.9 %copy-start.2 = (bf16[1024,124]{1,0:T(8,128)(2,1)S(1)}, bf16[1024,124]{1,0:T(8,128)(2,1)}, u32[]{:S(2)}) copy-start(bf16[1024,124]{1,0:T(8,128)(2,1)} %get-tuple-element.1044) | copy-start | bytes 761860 | tf_op jit(solution)/shard_map/while
  8.2 13.9 %copy-start.6 = (bf16[1024,256]{1,0:T(8,128)(2,1)S(1)}, bf16[1024,256]{1,0:T(8,128)(2,1)}, u32[]{:S(2)}) copy-start(bf16[1024,256]{1,0:T(8,128)(2,1)} %get-tuple-element.1042) | copy-start | bytes 1572868 | tf_op jit(solution)/shard_map/while
  8.2 13.9 %copy-start.10 = (s32[2,128]{1,0:T(2,128)S(1)}, s32[2,128]{1,0:T(2,128)}, u32[]{:S(2)}) copy-start(s32[2,128]{1,0:T(2,128)} %get-tuple-element.1043) | copy-start | bytes 3076 | tf_op jit(solution)/shard_map/while
  9.3 4.4 %collective-permute-start = (bf16[128,256]{0,1:T(8,128)(2,1)S(1)}, bf16[128,256]{0,1:T(8,128)(2,1)S(1)}, u32[]{:S(2)}, u32[]{:S(2)}) collective-permute-start(bf16[128,256]{0,1:T(8,128)(2,1)S(1)} %bitcast_select_fusion.4), channel_id=1, source_target_pairs={{0,1},{1,2},{2,3},{3,0},{4,5},{5,6},{6,7},{7,4},{8,9},{9,10},{10,1... | collective-permute-start | bytes 196616 | tf_op jit(solution)/shard_map/while/body/eval_jaxpr/ppermute | solution.py:124
  13.7 3.7 collective-permute-start.1
  17.4 3.7 collective-permute-start.2
  24.5 3.7 collective-permute-start.3
  28.2 13.2 %copy-start = (bf16[1024,256]{1,0:T(8,128)(2,1)S(1)}, bf16[1024,256]{1,0:T(8,128)(2,1)}, u32[]{:S(2)}) copy-start(bf16[1024,256]{1,0:T(8,128)(2,1)} %get-tuple-element.1041) | copy-start | bytes 1572868 | tf_op jit(solution)/shard_map/while
  28.2 13.2 %copy-start.2 = (bf16[1024,124]{1,0:T(8,128)(2,1)S(1)}, bf16[1024,124]{1,0:T(8,128)(2,1)}, u32[]{:S(2)}) copy-start(bf16[1024,124]{1,0:T(8,128)(2,1)} %get-tuple-element.1044) | copy-start | bytes 761860 | tf_op jit(solution)/shard_map/while
  28.2 13.2 %copy-start.6 = (bf16[1024,256]{1,0:T(8,128)(2,1)S(1)}, bf16[1024,256]{1,0:T(8,128)(2,1)}, u32[]{:S(2)}) copy-start(bf16[1024,256]{1,0:T(8,128)(2,1)} %get-tuple-element.1042) | copy-start | bytes 1572868 | tf_op jit(solution)/shard_map/while
  28.2 13.2 %copy-start.10 = (s32[2,128]{1,0:T(2,128)S(1)}, s32[2,128]{1,0:T(2,128)}, u32[]{:S(2)}) copy-start(s32[2,128]{1,0:T(2,128)} %get-tuple-element.1043) | copy-start | bytes 3076 | tf_op jit(solution)/shard_map/while
  29.3 3.7 %collective-permute-start = (bf16[128,256]{0,1:T(8,128)(2,1)S(1)}, bf16[128,256]{0,1:T(8,128)(2,1)S(1)}, u32[]{:S(2)}, u32[]{:S(2)}) collective-permute-start(bf16[128,256]{0,1:T(8,128)(2,1)S(1)} %bitcast_select_fusion.4), channel_id=1, source_target_pairs={{0,1},{1,2},{2,3},{3,0},{4,5},{5,6},{6,7},{7,4},{8,9},{9,10},{10,1... | collective-permute-start | bytes 196616 | tf_op jit(solution)/shard_map/while/body/eval_jaxpr/ppermute | solution.py:124
  33.0 3.7 collective-permute-start.1
  36.7 3.7 collective-permute-start.2
  43.8 6.2 %collective-permute-start.3 = (bf16[128,256]{0,1:T(8,128)(2,1)S(1)}, bf16[128,256]{0,1:T(8,128)(2,1)S(1)}, u32[]{:S(2)}, u32[]{:S(2)}) collective-permute-start(bf16[128,256]{0,1:T(8,128)(2,1)S(1)} %get-tuple-element.1100), channel_id=1, source_target_pairs={{0,4},{1,5},{2,6},{3,7},{8,12},{9,13},{10,14},{11,15},{16,20},{17,... | collective-permute-start | bytes 196616 | tf_op jit(solution)/shard_map/while/body/eval_jaxpr/ppermute | solution.py:12
  50.0 13.2 %copy-start = (bf16[1024,256]{1,0:T(8,128)(2,1)S(1)}, bf16[1024,256]{1,0:T(8,128)(2,1)}, u32[]{:S(2)}) copy-start(bf16[1024,256]{1,0:T(8,128)(2,1)} %get-tuple-element.1041) | copy-start | bytes 1572868 | tf_op jit(solution)/shard_map/while
  50.0 13.2 %copy-start.2 = (bf16[1024,124]{1,0:T(8,128)(2,1)S(1)}, bf16[1024,124]{1,0:T(8,128)(2,1)}, u32[]{:S(2)}) copy-start(bf16[1024,124]{1,0:T(8,128)(2,1)} %get-tuple-element.1044) | copy-start | bytes 761860 | tf_op jit(solution)/shard_map/while
  50.0 13.2 %copy-start.6 = (bf16[1024,256]{1,0:T(8,128)(2,1)S(1)}, bf16[1024,256]{1,0:T(8,128)(2,1)}, u32[]{:S(2)}) copy-start(bf16[1024,256]{1,0:T(8,128)(2,1)} %get-tuple-element.1042) | copy-start | bytes 1572868 | tf_op jit(solution)/shard_map/while
  50.0 13.2 %copy-start.10 = (s32[2,128]{1,0:T(2,128)S(1)}, s32[2,128]{1,0:T(2,128)}, u32[]{:S(2)}) copy-start(s32[2,128]{1,0:T(2,128)} %get-tuple-element.1043) | copy-start | bytes 3076 | tf_op jit(solution)/shard_map/while
  51.1 3.7 %collective-permute-start = (bf16[128,256]{0,1:T(8,128)(2,1)S(1)}, bf16[128,256]{0,1:T(8,128)(2,1)S(1)}, u32[]{:S(2)}, u32[]{:S(2)}) collective-permute-start(bf16[128,256]{0,1:T(8,128)(2,1)S(1)} %bitcast_select_fusion.4), channel_id=1, source_target_pairs={{0,1},{1,2},{2,3},{3,0},{4,5},{5,6},{6,7},{7,4},{8,9},{9,10},{10,1... | collective-permute-start | bytes 196616 | tf_op jit(solution)/shard_map/while/body/eval_jaxpr/ppermute | solution.py:124
  54.8 3.7 collective-permute-start.1
  58.5 3.7 collective-permute-start.2
  63.3 8.6 %collective-permute-start.3 = (bf16[128,256]{0,1:T(8,128)(2,1)S(1)}, bf16[128,256]{0,1:T(8,128)(2,1)S(1)}, u32[]{:S(2)}, u32[]{:S(2)}) collective-permute-start(bf16[128,256]{0,1:T(8,128)(2,1)S(1)} %get-tuple-element.1100), channel_id=1, source_target_pairs={{0,4},{1,5},{2,6},{3,7},{8,12},{9,13},{10,14},{11,15},{16,20},{17,... | collective-permute-start | bytes 196616 | tf_op jit(solution)/shard_map/while/body/eval_jaxpr/ppermute | solution.py:12
  73.1 78.3 %all-reduce.2.cloned.1.call-start = ((), (), s32[]{:S(2)}) async-start(), calls=%async_computation.2 | async-start | bytes 524288 | tf_op jit(solution)/shard_map/while/body/eval_jaxpr/psum | solution.py:159
  154.3 6.2 %collective-permute-start.4 = (bf16[128,256]{1,0:T(8,128)(2,1)S(1)}, bf16[128,256]{1,0:T(8,128)(2,1)S(1)}, u32[]{:S(2)}, u32[]{:S(2)}) collective-permute-start(bf16[128,256]{1,0:T(8,128)(2,1)S(1)} %fusion.74), channel_id=1, source_target_pairs={{4,0},{5,1},{6,2},{7,3},{12,8},{13,9},{14,10},{15,11},{20,16},{21,... | collective-permute-start | bytes 196616 | tf_op jit(solution)/shard_map/while/body/eval_jaxpr/ppermute | solution.py:12
  161.1 75.0 %all-reduce.2.cloned.1.call-start = ((), (), s32[]{:S(2)}) async-start(), calls=%async_computation.2 | async-start | bytes 524288 | tf_op jit(solution)/shard_map/while/body/eval_jaxpr/psum | solution.py:159
  239.1 6.2 %collective-permute-start.4 = (bf16[128,256]{1,0:T(8,128)(2,1)S(1)}, bf16[128,256]{1,0:T(8,128)(2,1)S(1)}, u32[]{:S(2)}, u32[]{:S(2)}) collective-permute-start(bf16[128,256]{1,0:T(8,128)(2,1)S(1)} %fusion.74), channel_id=1, source_target_pairs={{4,0},{5,1},{6,2},{7,3},{12,8},{13,9},{14,10},{15,11},{20,16},{21,... | collective-permute-start | bytes 196616 | tf_op jit(solution)/shard_map/while/body/eval_jaxpr/ppermute | solution.py:12
  245.9 75.0 %all-reduce.2.cloned.1.call-start = ((), (), s32[]{:S(2)}) async-start(), calls=%async_computation.2 | async-start | bytes 524288 | tf_op jit(solution)/shard_map/while/body/eval_jaxpr/psum | solution.py:159
  284.6 4.2 %copy-start.7 = (bf16[128,124]{1,0:T(8,128)(2,1)S(1)}, bf16[128,124]{1,0:T(8,128)(2,1)}, u32[]{:S(2)}) copy-start(bf16[128,124]{1,0:T(8,128)(2,1)} %reshape.252) | copy-start | bytes 95236 | tf_op jit(solution)/shard_map/while/body/eval_jaxpr/cond
  323.9 6.2 %collective-permute-start.4 = (bf16[128,256]{1,0:T(8,128)(2,1)S(1)}, bf16[128,256]{1,0:T(8,128)(2,1)S(1)}, u32[]{:S(2)}, u32[]{:S(2)}) collective-permute-start(bf16[128,256]{1,0:T(8,128)(2,1)S(1)} %fusion.74), channel_id=1, source_target_pairs={{4,0},{5,1},{6,2},{7,3},{12,8},{13,9},{14,10},{15,11},{20,16},{21,... | collective-permute-start | bytes 196616 | tf_op jit(solution)/shard_map/while/body/eval_jaxpr/ppermute | solution.py:12
  330.7 33.1 %reduce-scatter.2.cloned.1.call-start = ((), (), s32[]{:S(2)}) async-start(), calls=%async_computation.1 | async-start | bytes 1638400 | tf_op jit(solution)/shard_map/reduce_scatter | solution.py:185
  (13 other events, 29.3 us)
Sparse Core Ops, SparseCore 0:
  79.6 71.7 all-reduce.1
  205.1 31.0 all-reduce.1
  289.9 31.0 all-reduce.1
Sparse Core Ops, SparseCore 1:
  333.5 30.3 reduce-scatter.1
